TPU v7x, 128 devices: a whole 4x4x4 slice. The times are simulated.
128 devices in a mesh: ctx: 32 (over y, z, core), tp: 4 (over x).
Axes of the slice: x: 4, y: 4, z: 4, core: 2. Of those that a mesh axis runs over, the one named last changes fastest.
Arguments:
- query: bfloat16 [16384, 6144], P('ctx', 'tp'), may hold values from -6 to 6
- key_in: bfloat16 [16384, 6144], P('ctx', 'tp'), may hold values from -6 to 6
- value_in: bfloat16 [16384, 6144], P('ctx', 'tp'), may hold values from -6 to 6
- dout: bfloat16 [16384, 6144], P('ctx', 'tp'), may hold values from -0.5 to 0.5
- summary_offset: int32 [4], replicated, may hold values from 0 to 31
Outputs:
- grad_query: bfloat16 [16384, 6144], P(('ctx', 'tp'))
- grad_key: bfloat16 [16384, 6144], P(('ctx', 'tp'))
- grad_value: bfloat16 [16384, 6144], P(('ctx', 'tp'))
Inputs may be any that keep to these rules, and one draw needn't show every extreme that they name: Summary block s is block s * 32 + summary_offset[s].
All inputs are finite; a program needn't handle non-finite values.
Results may differ from a plain program's by a relative error of at most 0.014.
Values may be sent and summed in bfloat16 or wider, within the bound.
No kernel may reach another device: no remote copies, remote signals or barrier semaphores. Data moves between devices by JAX's collectives and lax.ppermute only.
A program may use at most 128 MiB of HBM per device.

v0:
```python
import jax
import jax.numpy as jnp
from jax import lax
from jax.sharding import PartitionSpec as P

HDIM = 128
BLOCK = 128
BAND = 8
STRIDE = 32
REACH = 2


def passed_along(value, axis, steps):
    count = lax.axis_size(axis)
    leading, last = (max(0, -steps), min(count, count - steps))
    return lax.ppermute(value, axis, [(source, source + steps) for source in range(leading, last)])


def broadcast(value, axis, source):
    kept = jnp.where(lax.axis_index(axis) == source, value, 0).astype(value.dtype)
    return lax.psum(kept, axis)


def band_mask(query_tok, key_tok):
    return (
        (key_tok >= 0)
        & (key_tok <= query_tok)
        & (key_tok // BLOCK >= query_tok // BLOCK - (BAND - 1))
    )


def column(array, start):
    return lax.dynamic_slice_in_dim(array, start, HDIM, 1)


def in_summary(tokens, groups):
    return jnp.any((tokens // BLOCK)[:, None] == groups[None, :], axis=1)


def on_device(query, key_in, value_in, dout, summary_offset):
    rows, width = query.shape
    heads_here = width // HDIM
    me = lax.axis_index("ctx")
    n_ctx = lax.axis_size("ctx")
    scale = HDIM ** (-0.5)
    n_sum = summary_offset.shape[0]
    groups = jnp.arange(n_sum, dtype=jnp.int32) * STRIDE + summary_offset
    owner = groups * BLOCK // rows
    local_start = groups * BLOCK - owner * rows
    within = jnp.arange(BLOCK, dtype=jnp.int32)
    tile_rows = (local_start[:, None] + within[None, :]).reshape(-1)
    sum_tok = (groups[:, None] * BLOCK + within[None, :]).reshape(-1)
    sum_owner = jnp.repeat(owner, BLOCK)
    mine = (sum_owner == me)[:, None]

    def fetch(distance):
        return passed_along((key_in, value_in), "ctx", distance)

    fetched = [fetch(distance) for distance in range(REACH, 0, -1)]
    ext_k = jnp.concatenate([piece[0] for piece in fetched] + [key_in], axis=0)
    ext_v = jnp.concatenate([piece[1] for piece in fetched] + [value_in], axis=0)

    def fill(index, carry):
        start = local_start[index]
        tile = (
            lax.dynamic_slice_in_dim(key_in, start, BLOCK, 0),
            lax.dynamic_slice_in_dim(value_in, start, BLOCK, 0),
        )
        got_k, got_v = (
            broadcast(tile[0], "ctx", owner[index]),
            broadcast(tile[1], "ctx", owner[index]),
        )
        return (
            lax.dynamic_update_slice_in_dim(carry[0], got_k, index * BLOCK, 0),
            lax.dynamic_update_slice_in_dim(carry[1], got_v, index * BLOCK, 0),
        )

    empty = jnp.zeros((n_sum * BLOCK, width), jnp.bfloat16)
    sum_k, sum_v = lax.fori_loop(0, n_sum, fill, (empty, empty))
    key_all = jnp.concatenate([ext_k, sum_k], axis=0)
    value_all = jnp.concatenate([ext_v, sum_v], axis=0)
    query_tok = me * rows + jnp.arange(rows, dtype=jnp.int32)
    ext_tok = (me - REACH) * rows + jnp.arange((REACH + 1) * rows, dtype=jnp.int32)
    elsewhere = in_summary(ext_tok, groups) & (ext_tok < me * rows)
    band_part = (
        band_mask(query_tok[:, None], ext_tok[None, :]) & jnp.logical_not(elsewhere)[None, :]
    )
    sum_block = (sum_tok // BLOCK)[None, :]
    query_block = (query_tok // BLOCK)[:, None]
    before_band = sum_block < query_block - (BAND - 1)
    inside_band = (
        (sum_block >= query_block - (BAND - 1))
        & (sum_block <= query_block)
        & (sum_owner != me)[None, :]
    )
    summary_ok = before_band | inside_band
    allowed = jnp.concatenate([band_part, summary_ok], axis=1)
    first_key = REACH * rows
    kept = key_all.shape[0] - first_key

    def own_head(head, carry):
        grad_q, grad_k, grad_v, lse_all, delta_all = carry
        start = head * HDIM
        rows_q = column(query, start)
        rows_do = column(dout, start)
        keys = column(key_all, start)
        values = column(value_all, start)
        scores = jnp.einsum("qd,kd->qk", rows_q, keys, preferred_element_type=jnp.float32) * scale
        top = jnp.max(jnp.where(allowed, scores, -jnp.inf), axis=1, keepdims=True)
        total = jnp.sum(jnp.where(allowed, jnp.exp(scores - top), 0.0), axis=1, keepdims=True)
        lse = top + jnp.log(total)
        prob = jnp.where(allowed, jnp.exp(scores - lse), 0.0)
        dprob = jnp.einsum("qd,kd->qk", rows_do, values, preferred_element_type=jnp.float32)
        delta = jnp.sum(prob * dprob, axis=1, keepdims=True)
        dscore = (prob * (dprob - delta)).astype(jnp.bfloat16)
        prob_low = prob.astype(jnp.bfloat16)
        head_q = (
            jnp.einsum("qk,kd->qd", dscore, keys, preferred_element_type=jnp.float32) * scale
        ).astype(jnp.bfloat16)
        head_k = (
            jnp.einsum(
                "qk,qd->kd", dscore[:, first_key:], rows_q, preferred_element_type=jnp.float32
            )
            * scale
        )
        head_v = jnp.einsum(
            "qk,qd->kd", prob_low[:, first_key:], rows_do, preferred_element_type=jnp.float32
        )
        grad_q = lax.dynamic_update_slice_in_dim(grad_q, head_q, start, 1)
        grad_k = lax.dynamic_update_slice_in_dim(grad_k, head_k, start, 1)
        grad_v = lax.dynamic_update_slice_in_dim(grad_v, head_v, start, 1)
        lse_all = lax.dynamic_update_slice_in_dim(lse_all, lse.reshape(1, rows), head, 0)
        delta_all = lax.dynamic_update_slice_in_dim(delta_all, delta.reshape(1, rows), head, 0)
        return (grad_q, grad_k, grad_v, lse_all, delta_all)

    start_carry = (
        jnp.zeros((rows, width), jnp.bfloat16),
        jnp.zeros((kept, width), jnp.float32),
        jnp.zeros((kept, width), jnp.float32),
        jnp.zeros((heads_here, rows), jnp.float32),
        jnp.zeros((heads_here, rows), jnp.float32),
    )
    grad_q, grad_k, grad_v, lse_all, delta_all = lax.fori_loop(0, heads_here, own_head, start_carry)

    def remote_terms(later_q, later_do, later_lse, later_delta, later_mask):

        def remote_head(head, carry):
            acc_k, acc_v = carry
            start = head * HDIM
            rows_q = column(later_q, start)
            rows_do = column(later_do, start)
            keys = column(key_in, start)
            values = column(value_in, start)
            lse = lax.dynamic_slice_in_dim(later_lse, head, 1, 0).reshape(rows, 1)
            delta = lax.dynamic_slice_in_dim(later_delta, head, 1, 0).reshape(rows, 1)
            scores = (
                jnp.einsum("qd,kd->qk", rows_q, keys, preferred_element_type=jnp.float32) * scale
            )
            prob = jnp.where(later_mask, jnp.exp(scores - lse), 0.0)
            dprob = jnp.einsum("qd,kd->qk", rows_do, values, preferred_element_type=jnp.float32)
            dscore = (prob * (dprob - delta)).astype(jnp.bfloat16)
            prob_low = prob.astype(jnp.bfloat16)
            head_k = (
                jnp.einsum("qk,qd->kd", dscore, rows_q, preferred_element_type=jnp.float32) * scale
            )
            head_v = jnp.einsum("qk,qd->kd", prob_low, rows_do, preferred_element_type=jnp.float32)
            acc_k = lax.dynamic_update_slice_in_dim(acc_k, column(acc_k, start) + head_k, start, 1)
            acc_v = lax.dynamic_update_slice_in_dim(acc_v, column(acc_v, start) + head_v, start, 1)
            return (acc_k, acc_v)

        return remote_head

    local_k = grad_k[:rows]
    local_v = grad_v[:rows]
    local_tok = me * rows + jnp.arange(rows, dtype=jnp.int32)
    local_plain = jnp.logical_not(in_summary(local_tok, groups))[None, :]
    for distance in range(1, REACH + 1):
        inputs = passed_along((query, dout), "ctx", -distance)
        stats = passed_along((lse_all, delta_all), "ctx", -distance)
        (later_q, later_do), (later_lse, later_delta) = (inputs, stats)
        later_tok = (me + distance) * rows + jnp.arange(rows, dtype=jnp.int32)
        later_mask = (
            band_mask(later_tok[:, None], local_tok[None, :])
            & (later_tok < n_ctx * rows)[:, None]
            & local_plain
        )
        local_k, local_v = lax.fori_loop(
            0,
            heads_here,
            remote_terms(later_q, later_do, later_lse, later_delta, later_mask),
            (local_k, local_v),
        )
    summary_k = grad_k[rows:]
    summary_v = grad_v[rows:]
    total_k, total_v = lax.psum((summary_k, summary_v), "ctx")
    local_k = local_k.at[tile_rows].add(jnp.where(mine, total_k, 0.0))
    local_v = local_v.at[tile_rows].add(jnp.where(mine, total_v, 0.0))
    moved = (
        lax.all_to_all(grad_q, "tp", split_axis=0, concat_axis=1, tiled=True),
        lax.all_to_all(local_k.astype(jnp.bfloat16), "tp", split_axis=0, concat_axis=1, tiled=True),
        lax.all_to_all(local_v.astype(jnp.bfloat16), "tp", split_axis=0, concat_axis=1, tiled=True),
    )
    return (moved[0], moved[1], moved[2])


def solution(mesh):
    return jax.shard_map(
        on_device,
        mesh=mesh,
        in_specs=(P("ctx", "tp"), P("ctx", "tp"), P("ctx", "tp"), P("ctx", "tp"), P()),
        out_specs=(P(("ctx", "tp"), None), P(("ctx", "tp"), None), P(("ctx", "tp"), None)),
        check_vma=False,
    )
```

profile of v0, /device:TPU:8, one launch (start us, length us, event | category | flops | bytes accessed | tf_op | source)
XLA Modules:
  0.0 977.3 jit_solution(13444294860501639880)
XLA Ops:
  8.0 3.8 collective-permute-start
  13.8 3.8 collective-permute-start.2
  21.0 4.3 collective-permute-start.6
  28.9 20.7 %collective-permute-done = bf16[512,1536]{1,0:T(8,128)(2,1)} collective-permute-done((bf16[512,1536]{1,0:T(8,128)(2,1)}, bf16[512,1536]{1,0:T(8,128)(2,1)}, u32[]{:S(2)}, u32[]{:S(2)}) %collective-permute-start) | collective-permute-done | bytes 1572896 | tf_op jit(solution)/shard_map/ppermute | solution.py:16
  49.6 3.7 collective-permute-start.10
  53.3 27.9 %collective-permute-done.1 = bf16[512,1536]{1,0:T(8,128)(2,1)} collective-permute-done((bf16[512,1536]{1,0:T(8,128)(2,1)}, bf16[512,1536]{1,0:T(8,128)(2,1)}, u32[]{:S(2)}, u32[]{:S(2)}) %collective-permute-start.1) | collective-permute-done | bytes 1572896 | tf_op jit(solution)/shard_map/ppermute | solution.py:16
  85.6 458.6 %while.70 = (s32[]{:T(128)}, bf16[512,1536]{1,0:T(8,128)(2,1)}, bf16[512,1536]{1,0:T(8,128)(2,1)}, s32[4]{0:T(128)S(1)}, s32[4]{0:T(128)S(1)}, /*index=5*/bf16[5...) while((s32[]{:T(128)}, bf16[512,1536]{1,0:T(8,128)(2,1)}, ...), condition=%wide.region_3.4_spmd, body=%wide.region_0.3_spmd.sunk | while | flops 786445 | bytes 7864643 | solution.py:79
  91.5 108.0 %all-reduce.9.cloned.1.call-done = (bf16[128,1536]{1,0:T(8,128)(2,1)}, bf16[128,1536]{1,0:T(8,128)(2,1)}) async-done(((bf16[128,1536]{1,0:T(8,128)(2,1)}, bf16[128,1536]{1,0:T(8,128)(2,1)}), (bf16[128,1536]{1,0:T(8,128)(2,1)}, bf16[128,1536]{1,0:T(8,128)(2,1)})) %all-reduce.9.cloned.1.call-update) | async-done | bytes 786448 | tf_op jit(solution)/shard_map/while/body/eval_jaxpr/psum | solution.py:21
  208.9 104.3 %all-reduce.9.cloned.1.call-done = (bf16[128,1536]{1,0:T(8,128)(2,1)}, bf16[128,1536]{1,0:T(8,128)(2,1)}) async-done(((bf16[128,1536]{1,0:T(8,128)(2,1)}, bf16[128,1536]{1,0:T(8,128)(2,1)}), (bf16[128,1536]{1,0:T(8,128)(2,1)}, bf16[128,1536]{1,0:T(8,128)(2,1)})) %all-reduce.9.cloned.1.call-update) | async-done | bytes 786448 | tf_op jit(solution)/shard_map/while/body/eval_jaxpr/psum | solution.py:21
  322.6 104.3 %all-reduce.9.cloned.1.call-done = (bf16[128,1536]{1,0:T(8,128)(2,1)}, bf16[128,1536]{1,0:T(8,128)(2,1)}) async-done(((bf16[128,1536]{1,0:T(8,128)(2,1)}, bf16[128,1536]{1,0:T(8,128)(2,1)}), (bf16[128,1536]{1,0:T(8,128)(2,1)}, bf16[128,1536]{1,0:T(8,128)(2,1)})) %all-reduce.9.cloned.1.call-update) | async-done | bytes 786448 | tf_op jit(solution)/shard_map/while/body/eval_jaxpr/psum | solution.py:21
  436.3 104.3 %all-reduce.9.cloned.1.call-done = (bf16[128,1536]{1,0:T(8,128)(2,1)}, bf16[128,1536]{1,0:T(8,128)(2,1)}) async-done(((bf16[128,1536]{1,0:T(8,128)(2,1)}, bf16[128,1536]{1,0:T(8,128)(2,1)}), (bf16[128,1536]{1,0:T(8,128)(2,1)}, bf16[128,1536]{1,0:T(8,128)(2,1)})) %all-reduce.9.cloned.1.call-update) | async-done | bytes 786448 | tf_op jit(solution)/shard_map/while/body/eval_jaxpr/psum | solution.py:21
  544.2 6.5 pad_maximum_fusion
  550.7 4.9 pad_maximum_fusion.1
  563.6 162.5 %while.71 = (s32[]{:T(128)}, bf16[512,1536]{1,0:T(8,128)(2,1)}, f32[1024,1536]{1,0:T(8,128)}, f32[1024,1536]{1,0:T(8,128)}, f32[12,512]{1,0:T(8,128)S(1)}, /*ind...) while((s32[]{:T(128)}, bf16[512,1536]{1,0:T(8,128)(2,1)}, ...), condition=%wide.region_9.10_spmd, body=%wide.region_5.9_spmd.sunk | while | flops 1089731584 | bytes 42106048 | solution.py:143
  726.1 4.3 collective-permute-start.5
  733.5 6.2 fusion.102
  742.8 4.4 all-to-all-start
  755.6 75.6 %while.72 = (s32[]{:T(128)}, f32[512,1536]{1,0:T(8,128)}, f32[512,1536]{1,0:T(8,128)}, bf16[512,1536]{1,0:T(8,128)(2,1)}, bf16[512,1536]{1,0:T(8,128)(2,1)}, /*i...) while((s32[]{:T(128)}, f32[512,1536]{1,0:T(8,128)}, ...), condition=%wide.region_12.13_spmd.clone, body=%wide.region_11.12_spmd.clone.sunk | while | flops 272039936 | bytes 5007079 | solution.py:187
  831.2 75.5 %while.73 = (s32[]{:T(128)}, f32[512,1536]{1,0:T(8,128)}, f32[512,1536]{1,0:T(8,128)}, bf16[512,1536]{1,0:T(8,128)(2,1)}, bf16[512,1536]{1,0:T(8,128)(2,1)}, /*i...) while((s32[]{:T(128)}, f32[512,1536]{1,0:T(8,128)}, ...), condition=%wide.region_14.15_spmd.clone, body=%wide.region_13.14_spmd.clone.sunk | while | flops 272039936 | bytes 5007079 | solution.py:187
  906.7 10.6 %scatter_custom_fusion.1 = f32[512,1536]{1,0:T(8,128)} fusion(f32[512,1536]{1,0:T(8,128)} %get-tuple-element.718, s32[512]{0:T(512)S(1)} %bitcast.76, f32[512,1536]{1,0:T(8,128)} %get-tuple-element.910, f32[]{:T(128)} %constant.333.clone.1, pred[512]{0:T(512)(128)(4,1)S(1)} %broadcast_bitcast_fusion), kind=kCustom, calls=%fused_computation.91 | custom fusion | flops 1572864 | bytes 6292480 | tf_op jit(solution)/shard_map/scatter-add | solution.py:197
  920.7 4.7 all-to-all-start.2
  925.4 8.2 scatter_custom_fusion
  935.0 10.3 %all-to-all-done.2 = bf16[4,128,1536]{2,1,0:T(8,128)(2,1)} async-done(((bf16[4,128,1536]{2,1,0:T(8,128)(2,1)}), bf16[4,128,1536]{2,1,0:T(8,128)(2,1)}, u32[]{:S(2)}, u32[]{:S(2)}) %all-to-all-start.2) | async-done | bytes 1572896 | tf_op jit(solution)/shard_map/all_to_all | solution.py:201
  955.8 11.9 %all-to-all-done.1 = bf16[4,128,1536]{2,1,0:T(8,128)(2,1)S(1)} async-done(((bf16[4,128,1536]{2,1,0:T(8,128)(2,1)}), bf16[4,128,1536]{2,1,0:T(8,128)(2,1)S(1)}, u32[]{:S(2)}, u32[]{:S(2)}) %all-to-all-start.1) | async-done | bytes 1572896 | tf_op jit(solution)/shard_map/all_to_all | solution.py:200
  (313 shorter events, 393.7 us)
Async XLA Ops:
  8.0 41.6 %collective-permute-start = (bf16[512,1536]{1,0:T(8,128)(2,1)}, bf16[512,1536]{1,0:T(8,128)(2,1)}, u32[]{:S(2)}, u32[]{:S(2)}) collective-permute-start(bf16[512,1536]{1,0:T(8,128)(2,1)} %param.14), channel_id=1, source_target_pairs={{0,8},{4,12},{8,16},{12,20},{16,24},{20,28},{24,32},{28,36},{32,40... | collective-permute-start | bytes 4718600 | tf_op jit(solution)/shard_map/ppermute | solution.py:16
  11.8 69.3 %collective-permute-start.1 = (bf16[512,1536]{1,0:T(8,128)(2,1)}, bf16[512,1536]{1,0:T(8,128)(2,1)}, u32[]{:S(2)}, u32[]{:S(2)}) collective-permute-start(bf16[512,1536]{1,0:T(8,128)(2,1)} %param.14), channel_id=1, source_target_pairs={{0,4},{4,8},{8,12},{12,16},{16,20},{20,24},{24,28},{28,32},{32,36}... | collective-permute-start | bytes 4718600 | tf_op jit(solution)/shard_map/ppermute | solution.py:16
  13.8 536.9 %collective-permute-start.2 = (bf16[512,1536]{1,0:T(8,128)(2,1)}, bf16[512,1536]{1,0:T(8,128)(2,1)}, u32[]{:S(2)}, u32[]{:S(2)}) collective-permute-start(bf16[512,1536]{1,0:T(8,128)(2,1)} %param.15), channel_id=1, source_target_pairs={{0,8},{4,12},{8,16},{12,20},{16,24},{20,28},{24,32},{28,36},{32,40... | collective-permute-start | bytes 4718600 | tf_op jit(solution)/shard_map/ppermute | solution.py:16
  17.6 533.0 %collective-permute-start.3 = (bf16[512,1536]{1,0:T(8,128)(2,1)}, bf16[512,1536]{1,0:T(8,128)(2,1)}, u32[]{:S(2)}, u32[]{:S(2)}) collective-permute-start(bf16[512,1536]{1,0:T(8,128)(2,1)} %param.15), channel_id=1, source_target_pairs={{0,4},{4,8},{8,12},{12,16},{16,20},{20,24},{24,28},{28,32},{32,36}... | collective-permute-start | bytes 4718600 | tf_op jit(solution)/shard_map/ppermute | solution.py:16
  21.0 728.7 %collective-permute-start.6 = (bf16[512,1536]{1,0:T(8,128)(2,1)}, bf16[512,1536]{1,0:T(8,128)(2,1)}, u32[]{:S(2)}, u32[]{:S(2)}) collective-permute-start(bf16[512,1536]{1,0:T(8,128)(2,1)} %param.16), channel_id=1, source_target_pairs={{4,0},{8,4},{12,8},{16,12},{20,16},{24,20},{28,24},{32,28},{36,32}... | collective-permute-start | bytes 4718600 | tf_op jit(solution)/shard_map/ppermute | solution.py:16
  27.3 58.3 %copy-start.2 = (bf16[512,1536]{1,0:T(8,128)(2,1)S(1)}, bf16[512,1536]{1,0:T(8,128)(2,1)}, u32[]{:S(2)}) copy-start(bf16[512,1536]{1,0:T(8,128)(2,1)} %param.15) | copy-start | bytes 4718596
  49.6 781.6 %collective-permute-start.10 = (bf16[512,1536]{1,0:T(8,128)(2,1)}, bf16[512,1536]{1,0:T(8,128)(2,1)}, u32[]{:S(2)}, u32[]{:S(2)}) collective-permute-start(bf16[512,1536]{1,0:T(8,128)(2,1)} %param.16), channel_id=1, source_target_pairs={{8,0},{12,4},{16,8},{20,12},{24,16},{28,20},{32,24},{36,28},{40,32... | collective-permute-start | bytes 4718600 | tf_op jit(solution)/shard_map/ppermute | solution.py:16
  81.2 666.6 %collective-permute-start.4 = (bf16[512,1536]{1,0:T(8,128)(2,1)}, bf16[512,1536]{1,0:T(8,128)(2,1)}, u32[]{:S(2)}, u32[]{:S(2)}) collective-permute-start(bf16[512,1536]{1,0:T(8,128)(2,1)} %param.13), channel_id=1, source_target_pairs={{4,0},{8,4},{12,8},{16,12},{20,16},{24,20},{28,24},{32,28},{36,32}... | collective-permute-start | bytes 4718600 | tf_op jit(solution)/shard_map/ppermute | solution.py:16
  85.6 113.9 %all-reduce.9.cloned.1.call-start = ((), (), s32[]{:S(2)}) async-start(), calls=%async_computation.4 | async-start | bytes 1572864 | tf_op jit(solution)/shard_map/while/body/eval_jaxpr/psum | solution.py:21
  203.0 110.2 %all-reduce.9.cloned.1.call-start = ((), (), s32[]{:S(2)}) async-start(), calls=%async_computation.4 | async-start | bytes 1572864 | tf_op jit(solution)/shard_map/while/body/eval_jaxpr/psum | solution.py:21
  316.7 110.2 %all-reduce.9.cloned.1.call-start = ((), (), s32[]{:S(2)}) async-start(), calls=%async_computation.4 | async-start | bytes 1572864 | tf_op jit(solution)/shard_map/while/body/eval_jaxpr/psum | solution.py:21
  430.5 110.2 %all-reduce.9.cloned.1.call-start = ((), (), s32[]{:S(2)}) async-start(), calls=%async_computation.4 | async-start | bytes 1572864 | tf_op jit(solution)/shard_map/while/body/eval_jaxpr/psum | solution.py:21
  544.2 6.5 copy-start.3
  726.1 26.0 %collective-permute-start.5 = (f32[12,512]{1,0:T(8,128)S(1)}, f32[12,512]{1,0:T(8,128)S(1)}, u32[]{:S(2)}, u32[]{:S(2)}) collective-permute-start(f32[12,512]{1,0:T(8,128)S(1)} %get-tuple-element.713), channel_id=1, source_target_pairs={{4,0},{8,4},{12,8},{16,12},{20,16},{24,20},{28,24},{32,28},{36,32}... | collective-permute-start | bytes 73736 | tf_op jit(solution)/shard_map/ppermute | solution.py:16
  730.4 25.2 %collective-permute-start.7 = (f32[12,512]{1,0:T(8,128)S(1)}, f32[12,512]{1,0:T(8,128)S(1)}, u32[]{:S(2)}, u32[]{:S(2)}) collective-permute-start(f32[12,512]{1,0:T(8,128)S(1)} %get-tuple-element.714), channel_id=1, source_target_pairs={{4,0},{8,4},{12,8},{16,12},{20,16},{24,20},{28,24},{32,28},{36,32}... | collective-permute-start | bytes 73736 | tf_op jit(solution)/shard_map/ppermute | solution.py:16
  733.4 6.3 copy-start.1
  742.8 177.9 %all-to-all-start = ((bf16[4,128,1536]{2,1,0:T(8,128)(2,1)}), bf16[4,128,1536]{2,1,0:T(8,128)(2,1)}, u32[]{:S(2)}, u32[]{:S(2)}) async-start(bf16[4,128,1536]{2,1,0:T(8,128)(2,1)} %bitcast.63), calls=%async_computation | async-start | bytes 3145728 | tf_op jit(solution)/shard_map/all_to_all | solution.py:199
  747.2 159.6 %all-reduce.7.cloned.1.call-start = ((), (), s32[]{:S(2)}) async-start(), calls=%async_computation.3 | async-start | bytes 12582912 | tf_op jit(solution)/shard_map/psum | solution.py:195
  747.8 83.4 %collective-permute-start.8 = (bf16[512,1536]{1,0:T(8,128)(2,1)}, bf16[512,1536]{1,0:T(8,128)(2,1)}, u32[]{:S(2)}, u32[]{:S(2)}) collective-permute-start(bf16[512,1536]{1,0:T(8,128)(2,1)} %param.13), channel_id=1, source_target_pairs={{8,0},{12,4},{16,8},{20,12},{24,16},{28,20},{32,24},{36,28},{40,32... | collective-permute-start | bytes 4718600 | tf_op jit(solution)/shard_map/ppermute | solution.py:16
  749.7 81.5 %collective-permute-start.11 = (f32[12,512]{1,0:T(8,128)S(1)}, f32[12,512]{1,0:T(8,128)S(1)}, u32[]{:S(2)}, u32[]{:S(2)}) collective-permute-start(f32[12,512]{1,0:T(8,128)S(1)} %get-tuple-element.714), channel_id=1, source_target_pairs={{8,0},{12,4},{16,8},{20,12},{24,16},{28,20},{32,24},{36,28},{40,32... | collective-permute-start | bytes 73736 | tf_op jit(solution)/shard_map/ppermute | solution.py:16
  752.1 79.1 %collective-permute-start.9 = (f32[12,512]{1,0:T(8,128)S(1)}, f32[12,512]{1,0:T(8,128)S(1)}, u32[]{:S(2)}, u32[]{:S(2)}) collective-permute-start(f32[12,512]{1,0:T(8,128)S(1)} %get-tuple-element.713), channel_id=1, source_target_pairs={{8,0},{12,4},{16,8},{20,12},{24,16},{28,20},{32,24},{36,28},{40,32... | collective-permute-start | bytes 73736 | tf_op jit(solution)/shard_map/ppermute | solution.py:16
  917.4 8.1 copy-start
  920.7 24.6 %all-to-all-start.2 = ((bf16[4,128,1536]{2,1,0:T(8,128)(2,1)}), bf16[4,128,1536]{2,1,0:T(8,128)(2,1)}, u32[]{:S(2)}, u32[]{:S(2)}) async-start(bf16[4,128,1536]{2,1,0:T(8,128)(2,1)} %bitcast.67), calls=%async_computation.2 | async-start | bytes 3145728 | tf_op jit(solution)/shard_map/all_to_all | solution.py:201
  945.3 22.4 %all-to-all-start.1 = ((bf16[4,128,1536]{2,1,0:T(8,128)(2,1)}), bf16[4,128,1536]{2,1,0:T(8,128)(2,1)S(1)}, u32[]{:S(2)}, u32[]{:S(2)}) async-start(bf16[4,128,1536]{2,1,0:T(8,128)(2,1)} %bitcast.68), calls=%async_computation.1 | async-start | bytes 3145728 | tf_op jit(solution)/shard_map/all_to_all | solution.py:200
Sparse Core Ops, SparseCore 0:
  91.6 107.8 all-reduce.8
  209.0 104.1 all-reduce.8
  322.7 104.1 all-reduce.8
  436.5 104.1 all-reduce.8
Sparse Core Ops, SparseCore 1:
  751.2 130.4 all-reduce.6
where the time goes:
time: 982 us; the launch traced here: 977 us
  waiting for transfers between devices  492 us (50%)
  matrix products  291 us (30%)
  other arithmetic  66.8 us (7%)
  starting transfers between devices  50.7 us (5%)
  local copies, waits for them, and re-layouts  49.6 us (5%)
  between operations  15.5 us (2%)
  loops' own time  11.1 us (1%)
    psum x4, waiting for transfers between devices, broadcast(): return lax.psum(kept, axis)  421 us
    dot_general x24, matrix products, remote_head(): jnp.einsum('qk,qd->kd', dscore, rows_q, preferred_element_type=jnp.float32)  61.8 us
    dot_general x24, matrix products, remote_head(): jnp.einsum('qk,qd->kd', prob_low, rows_do, preferred_element_type=jnp.flo...  50.9 us
    ppermute x12, waiting for transfers between devices, passed_along(): lax.ppermute(value, axis, [(source, source + steps) for source in range(l...  48.6 us
    ppermute x12, starting transfers between devices, passed_along(): lax.ppermute(value, axis, [(source, source + steps) for source in range(l...  38 us
    dot_general x24, matrix products, remote_head(): jnp.einsum('qd,kd->qk', rows_q, keys, preferred_element_type=jnp.float32)  37.9 us
    dot_general x12, matrix products, own_head(): jnp.einsum('qd,kd->qk', rows_do, values, preferred_element_type=jnp.float32)  32.6 us
    dot_general x12, matrix products, own_head(): jnp.einsum('qk,kd->qd', dscore, keys, preferred_element_type=jnp.float32)  28.9 us
  transfers between devices with their start and end apart: 20, of which 8 were waited for; matrix products, arithmetic and copies ran while one was open for 41% of the time, Pallas kernels for 0%

commit v1 on v0

--- a/solution.py
+++ b/solution.py
@@ -18,7 +18,7 @@
 
 def broadcast(value, axis, source):
     kept = jnp.where(lax.axis_index(axis) == source, value, 0).astype(value.dtype)
-    return lax.psum(kept, axis)
+    return jnp.sum(jax.lax.all_gather(kept, axis), 0)
 
 
 def band_mask(query_tok, key_tok):

time: 982 us -> 1090 us (1.11)
  waiting for transfers between devices: 492 us -> 556 us
  other arithmetic: 66.8 us -> 122 us
    all_gather x0 -> x8, waiting for transfers between devices: none -> 484 us  [broadcast(): return jnp.sum(jax.lax.all_gather(kept, axis), 0)]
    psum x4 -> x0, waiting for transfers between devices: 421 us -> none  [broadcast(): return lax.psum(kept, axis)]
    reduce_sum x0 -> x8, other arithmetic: none -> 52.9 us  [broadcast(): return jnp.sum(jax.lax.all_gather(kept, axis), 0)]
  transfers between devices with their start and end apart: 20 -> 24, of which waited for: 8 -> 12; matrix products, arithmetic and copies ran while one was open for 41% -> 42% of each run, Pallas kernels for 0% -> 0%
where the time goes in v1:
time: 1090 us
  waiting for transfers between devices  556 us (51%)
  matrix products  291 us (27%)
  other arithmetic  122 us (11%)
  starting transfers between devices  50.3 us (5%)
  local copies, waits for them, and re-layouts  41.7 us (4%)
  between operations  15.8 us (1%)
  loops' own time  11.1 us (1%)
    all_gather x8, waiting for transfers between devices, broadcast(): return jnp.sum(jax.lax.all_gather(kept, axis), 0)  484 us
    dot_general x24, matrix products, remote_head(): jnp.einsum('qk,qd->kd', dscore, rows_q, preferred_element_type=jnp.float32)  61.8 us
    reduce_sum x8, other arithmetic, broadcast(): return jnp.sum(jax.lax.all_gather(kept, axis), 0)  52.9 us
    dot_general x24, matrix products, remote_head(): jnp.einsum('qk,qd->kd', prob_low, rows_do, preferred_element_type=jnp.flo...  50.9 us
    ppermute x12, waiting for transfers between devices, passed_along(): lax.ppermute(value, axis, [(source, source + steps) for source in range(l...  48.6 us
    dot_general x24, matrix products, remote_head(): jnp.einsum('qd,kd->qk', rows_q, keys, preferred_element_type=jnp.float32)  37.9 us
    ppermute x12, starting transfers between devices, passed_along(): lax.ppermute(value, axis, [(source, source + steps) for source in range(l...  37.6 us
    dot_general x12, matrix products, own_head(): jnp.einsum('qd,kd->qk', rows_do, values, preferred_element_type=jnp.float32)  32.6 us
  transfers between devices with their start and end apart: 24, of which 12 were waited for; matrix products, arithmetic and copies ran while one was open for 42% of the time, Pallas kernels for 0%

profile of v1, /device:TPU:8, one launch (start us, length us, event | category | flops | bytes accessed | tf_op | source)
XLA Modules:
  0.0 1088.8 jit_solution(7967635833759064092)
XLA Ops:
  28.9 20.7 %collective-permute-done = bf16[512,1536]{1,0:T(8,128)(2,1)} collective-permute-done((bf16[512,1536]{1,0:T(8,128)(2,1)}, bf16[512,1536]{1,0:T(8,128)(2,1)}, u32[]{:S(2)}, u32[]{:S(2)}) %collective-permute-start) | collective-permute-done | bytes 1572896 | tf_op jit(solution)/shard_map/ppermute | solution.py:16
  53.3 27.9 %collective-permute-done.1 = bf16[512,1536]{1,0:T(8,128)(2,1)} collective-permute-done((bf16[512,1536]{1,0:T(8,128)(2,1)}, bf16[512,1536]{1,0:T(8,128)(2,1)}, u32[]{:S(2)}, u32[]{:S(2)}) %collective-permute-start.1) | collective-permute-done | bytes 1572896 | tf_op jit(solution)/shard_map/ppermute | solution.py:16
  85.8 569.4 %while.71 = (s32[]{:T(128)}, bf16[512,1536]{1,0:T(8,128)(2,1)}, bf16[512,1536]{1,0:T(8,128)(2,1)}, s32[4]{0:T(128)S(1)}, s32[4]{0:T(128)S(1)}, /*index=5*/bf16[5...) while((s32[]{:T(128)}, bf16[512,1536]{1,0:T(8,128)(2,1)}, ...), condition=%wide.region_3.4_spmd, body=%wide.region_0.3_spmd.sunk | while | flops 12582925 | bytes 106955128 | solution.py:79
  92.3 68.2 %all-gather.11.cloned.1.call-done = bf16[4096,1536]{1,0:T(8,128)(2,1)} async-done(((bf16[128,1536]{1,0:T(8,128)(2,1)}), bf16[4096,1536]{1,0:T(8,128)(2,1)}) %all-gather.11.cloned.1.call-update) | async-done | bytes 12582928 | tf_op jit(solution)/shard_map/while/body/eval_jaxpr/all_gather | solution.py:21
  160.5 6.6 reduce_sum.61
  167.1 58.6 %all-gather.9.cloned.1.call-done = bf16[4096,1536]{1,0:T(8,128)(2,1)} async-done(((bf16[128,1536]{1,0:T(8,128)(2,1)}), bf16[4096,1536]{1,0:T(8,128)(2,1)}) %all-gather.9.cloned.1.call-update) | async-done | bytes 12582928 | tf_op jit(solution)/shard_map/while/body/eval_jaxpr/all_gather | solution.py:21
  225.7 6.6 reduce_sum.60
  240.4 60.6 %all-gather.11.cloned.1.call-done = bf16[4096,1536]{1,0:T(8,128)(2,1)} async-done(((bf16[128,1536]{1,0:T(8,128)(2,1)}), bf16[4096,1536]{1,0:T(8,128)(2,1)}) %all-gather.11.cloned.1.call-update) | async-done | bytes 12582928 | tf_op jit(solution)/shard_map/while/body/eval_jaxpr/all_gather | solution.py:21
  301.0 6.6 reduce_sum.61
  307.6 58.5 %all-gather.9.cloned.1.call-done = bf16[4096,1536]{1,0:T(8,128)(2,1)} async-done(((bf16[128,1536]{1,0:T(8,128)(2,1)}), bf16[4096,1536]{1,0:T(8,128)(2,1)}) %all-gather.9.cloned.1.call-update) | async-done | bytes 12582928 | tf_op jit(solution)/shard_map/while/body/eval_jaxpr/all_gather | solution.py:21
  366.1 6.6 reduce_sum.60
  380.8 60.6 %all-gather.11.cloned.1.call-done = bf16[4096,1536]{1,0:T(8,128)(2,1)} async-done(((bf16[128,1536]{1,0:T(8,128)(2,1)}), bf16[4096,1536]{1,0:T(8,128)(2,1)}) %all-gather.11.cloned.1.call-update) | async-done | bytes 12582928 | tf_op jit(solution)/shard_map/while/body/eval_jaxpr/all_gather | solution.py:21
  441.4 6.6 reduce_sum.61
  448.0 58.5 %all-gather.9.cloned.1.call-done = bf16[4096,1536]{1,0:T(8,128)(2,1)} async-done(((bf16[128,1536]{1,0:T(8,128)(2,1)}), bf16[4096,1536]{1,0:T(8,128)(2,1)}) %all-gather.9.cloned.1.call-update) | async-done | bytes 12582928 | tf_op jit(solution)/shard_map/while/body/eval_jaxpr/all_gather | solution.py:21
  521.2 60.6 %all-gather.11.cloned.1.call-done = bf16[4096,1536]{1,0:T(8,128)(2,1)} async-done(((bf16[128,1536]{1,0:T(8,128)(2,1)}), bf16[4096,1536]{1,0:T(8,128)(2,1)}) %all-gather.11.cloned.1.call-update) | async-done | bytes 12582928 | tf_op jit(solution)/shard_map/while/body/eval_jaxpr/all_gather | solution.py:21
  581.8 6.6 reduce_sum.61
  588.4 58.6 %all-gather.9.cloned.1.call-done = bf16[4096,1536]{1,0:T(8,128)(2,1)} async-done(((bf16[128,1536]{1,0:T(8,128)(2,1)}), bf16[4096,1536]{1,0:T(8,128)(2,1)}) %all-gather.9.cloned.1.call-update) | async-done | bytes 12582928 | tf_op jit(solution)/shard_map/while/body/eval_jaxpr/all_gather | solution.py:21
  674.6 162.4 %while.72 = (s32[]{:T(128)}, bf16[512,1536]{1,0:T(8,128)(2,1)}, f32[1024,1536]{1,0:T(8,128)}, f32[1024,1536]{1,0:T(8,128)}, f32[12,512]{1,0:T(8,128)S(1)}, /*ind...) while((s32[]{:T(128)}, bf16[512,1536]{1,0:T(8,128)(2,1)}, ...), condition=%wide.region_9.10_spmd, body=%wide.region_5.9_spmd.sunk | while | flops 1089731584 | bytes 42106048 | solution.py:143
  866.0 75.6 %while.73 = (s32[]{:T(128)}, f32[512,1536]{1,0:T(8,128)}, f32[512,1536]{1,0:T(8,128)}, bf16[512,1536]{1,0:T(8,128)(2,1)}, bf16[512,1536]{1,0:T(8,128)(2,1)}, /*i...) while((s32[]{:T(128)}, f32[512,1536]{1,0:T(8,128)}, ...), condition=%wide.region_12.13_spmd.clone, body=%wide.region_11.12_spmd.clone.sunk | while | flops 272039936 | bytes 5007079 | solution.py:187
  941.6 75.5 %while.74 = (s32[]{:T(128)}, f32[512,1536]{1,0:T(8,128)}, f32[512,1536]{1,0:T(8,128)}, bf16[512,1536]{1,0:T(8,128)(2,1)}, bf16[512,1536]{1,0:T(8,128)(2,1)}, /*i...) while((s32[]{:T(128)}, f32[512,1536]{1,0:T(8,128)}, ...), condition=%wide.region_14.15_spmd.clone, body=%wide.region_13.14_spmd.clone.sunk | while | flops 272039936 | bytes 5007079 | solution.py:187
  1017.1 10.6 scatter_custom_fusion.1
  1035.6 8.5 scatter_custom_fusion
  1045.4 10.5 all-to-all-done.2
  1066.5 12.4 %all-to-all-done.1 = bf16[4,128,1536]{2,1,0:T(8,128)(2,1)S(1)} async-done(((bf16[4,128,1536]{2,1,0:T(8,128)(2,1)}), bf16[4,128,1536]{2,1,0:T(8,128)(2,1)S(1)}, u32[]{:S(2)}, u32[]{:S(2)}) %all-to-all-start.1) | async-done | bytes 1572896 | tf_op jit(solution)/shard_map/all_to_all | solution.py:200
  (337 shorter events, 447.5 us)
Async XLA Ops:
  8.0 41.6 %collective-permute-start = (bf16[512,1536]{1,0:T(8,128)(2,1)}, bf16[512,1536]{1,0:T(8,128)(2,1)}, u32[]{:S(2)}, u32[]{:S(2)}) collective-permute-start(bf16[512,1536]{1,0:T(8,128)(2,1)} %param.14), channel_id=1, source_target_pairs={{0,8},{4,12},{8,16},{12,20},{16,24},{20,28},{24,32},{28,36},{32,40... | collective-permute-start | bytes 4718600 | tf_op jit(solution)/shard_map/ppermute | solution.py:16
  11.8 69.3 %collective-permute-start.1 = (bf16[512,1536]{1,0:T(8,128)(2,1)}, bf16[512,1536]{1,0:T(8,128)(2,1)}, u32[]{:S(2)}, u32[]{:S(2)}) collective-permute-start(bf16[512,1536]{1,0:T(8,128)(2,1)} %param.14), channel_id=1, source_target_pairs={{0,4},{4,8},{8,12},{12,16},{16,20},{20,24},{24,28},{28,32},{32,36}... | collective-permute-start | bytes 4718600 | tf_op jit(solution)/shard_map/ppermute | solution.py:16
  13.8 647.9 %collective-permute-start.2 = (bf16[512,1536]{1,0:T(8,128)(2,1)}, bf16[512,1536]{1,0:T(8,128)(2,1)}, u32[]{:S(2)}, u32[]{:S(2)}) collective-permute-start(bf16[512,1536]{1,0:T(8,128)(2,1)} %param.15), channel_id=1, source_target_pairs={{0,8},{4,12},{8,16},{12,20},{16,24},{20,28},{24,32},{28,36},{32,40... | collective-permute-start | bytes 4718600 | tf_op jit(solution)/shard_map/ppermute | solution.py:16
  17.6 644.1 %collective-permute-start.3 = (bf16[512,1536]{1,0:T(8,128)(2,1)}, bf16[512,1536]{1,0:T(8,128)(2,1)}, u32[]{:S(2)}, u32[]{:S(2)}) collective-permute-start(bf16[512,1536]{1,0:T(8,128)(2,1)} %param.15), channel_id=1, source_target_pairs={{0,4},{4,8},{8,12},{12,16},{16,20},{20,24},{24,28},{28,32},{32,36}... | collective-permute-start | bytes 4718600 | tf_op jit(solution)/shard_map/ppermute | solution.py:16
  21.0 839.7 %collective-permute-start.6 = (bf16[512,1536]{1,0:T(8,128)(2,1)}, bf16[512,1536]{1,0:T(8,128)(2,1)}, u32[]{:S(2)}, u32[]{:S(2)}) collective-permute-start(bf16[512,1536]{1,0:T(8,128)(2,1)} %param.16), channel_id=1, source_target_pairs={{4,0},{8,4},{12,8},{16,12},{20,16},{24,20},{28,24},{32,28},{36,32}... | collective-permute-start | bytes 4718600 | tf_op jit(solution)/shard_map/ppermute | solution.py:16
  49.6 892.0 %collective-permute-start.10 = (bf16[512,1536]{1,0:T(8,128)(2,1)}, bf16[512,1536]{1,0:T(8,128)(2,1)}, u32[]{:S(2)}, u32[]{:S(2)}) collective-permute-start(bf16[512,1536]{1,0:T(8,128)(2,1)} %param.16), channel_id=1, source_target_pairs={{8,0},{12,4},{16,8},{20,12},{24,16},{28,20},{32,24},{36,28},{40,32... | collective-permute-start | bytes 4718600 | tf_op jit(solution)/shard_map/ppermute | solution.py:16
  81.2 776.8 %collective-permute-start.4 = (bf16[512,1536]{1,0:T(8,128)(2,1)}, bf16[512,1536]{1,0:T(8,128)(2,1)}, u32[]{:S(2)}, u32[]{:S(2)}) collective-permute-start(bf16[512,1536]{1,0:T(8,128)(2,1)} %param.13), channel_id=1, source_target_pairs={{4,0},{8,4},{12,8},{16,12},{20,16},{24,20},{28,24},{32,28},{36,32}... | collective-permute-start | bytes 4718600 | tf_op jit(solution)/shard_map/ppermute | solution.py:16
  85.8 74.7 %all-gather.11.cloned.1.call-start = ((), (), s32[]{:S(2)}) async-start(), calls=%async_computation.5 | async-start | bytes 12976128 | tf_op jit(solution)/shard_map/while/body/eval_jaxpr/all_gather | solution.py:21
  90.3 135.4 %all-gather.9.cloned.1.call-start = ((), (), s32[]{:S(2)}) async-start(), calls=%async_computation.4 | async-start | bytes 12976128 | tf_op jit(solution)/shard_map/while/body/eval_jaxpr/all_gather | solution.py:21
  233.9 67.1 %all-gather.11.cloned.1.call-start = ((), (), s32[]{:S(2)}) async-start(), calls=%async_computation.5 | async-start | bytes 12976128 | tf_op jit(solution)/shard_map/while/body/eval_jaxpr/all_gather | solution.py:21
  238.5 127.7 %all-gather.9.cloned.1.call-start = ((), (), s32[]{:S(2)}) async-start(), calls=%async_computation.4 | async-start | bytes 12976128 | tf_op jit(solution)/shard_map/while/body/eval_jaxpr/all_gather | solution.py:21
  374.3 67.1 %all-gather.11.cloned.1.call-start = ((), (), s32[]{:S(2)}) async-start(), calls=%async_computation.5 | async-start | bytes 12976128 | tf_op jit(solution)/shard_map/while/body/eval_jaxpr/all_gather | solution.py:21
  378.8 127.7 %all-gather.9.cloned.1.call-start = ((), (), s32[]{:S(2)}) async-start(), calls=%async_computation.4 | async-start | bytes 12976128 | tf_op jit(solution)/shard_map/while/body/eval_jaxpr/all_gather | solution.py:21
  514.7 67.1 %all-gather.11.cloned.1.call-start = ((), (), s32[]{:S(2)}) async-start(), calls=%async_computation.5 | async-start | bytes 12976128 | tf_op jit(solution)/shard_map/while/body/eval_jaxpr/all_gather | solution.py:21
  519.2 127.8 %all-gather.9.cloned.1.call-start = ((), (), s32[]{:S(2)}) async-start(), calls=%async_computation.4 | async-start | bytes 12976128 | tf_op jit(solution)/shard_map/while/body/eval_jaxpr/all_gather | solution.py:21
  837.0 26.1 %collective-permute-start.5 = (f32[12,512]{1,0:T(8,128)S(1)}, f32[12,512]{1,0:T(8,128)S(1)}, u32[]{:S(2)}, u32[]{:S(2)}) collective-permute-start(f32[12,512]{1,0:T(8,128)S(1)} %get-tuple-element.734), channel_id=1, source_target_pairs={{4,0},{8,4},{12,8},{16,12},{20,16},{24,20},{28,24},{32,28},{36,32}... | collective-permute-start | bytes 73736 | tf_op jit(solution)/shard_map/ppermute | solution.py:16
  841.2 24.7 %collective-permute-start.7 = (f32[12,512]{1,0:T(8,128)S(1)}, f32[12,512]{1,0:T(8,128)S(1)}, u32[]{:S(2)}, u32[]{:S(2)}) collective-permute-start(f32[12,512]{1,0:T(8,128)S(1)} %get-tuple-element.735), channel_id=1, source_target_pairs={{4,0},{8,4},{12,8},{16,12},{20,16},{24,20},{28,24},{32,28},{36,32}... | collective-permute-start | bytes 73736 | tf_op jit(solution)/shard_map/ppermute | solution.py:16
  853.0 178.0 %all-to-all-start = ((bf16[4,128,1536]{2,1,0:T(8,128)(2,1)}), bf16[4,128,1536]{2,1,0:T(8,128)(2,1)}, u32[]{:S(2)}, u32[]{:S(2)}) async-start(bf16[4,128,1536]{2,1,0:T(8,128)(2,1)} %bitcast.8), calls=%async_computation | async-start | bytes 3145728 | tf_op jit(solution)/shard_map/all_to_all | solution.py:199
  857.4 159.7 %all-reduce.3.cloned.1.call-start = ((), (), s32[]{:S(2)}) async-start(), calls=%async_computation.3 | async-start | bytes 12582912 | tf_op jit(solution)/shard_map/psum | solution.py:195
  858.0 83.5 %collective-permute-start.8 = (bf16[512,1536]{1,0:T(8,128)(2,1)}, bf16[512,1536]{1,0:T(8,128)(2,1)}, u32[]{:S(2)}, u32[]{:S(2)}) collective-permute-start(bf16[512,1536]{1,0:T(8,128)(2,1)} %param.13), channel_id=1, source_target_pairs={{8,0},{12,4},{16,8},{20,12},{24,16},{28,20},{32,24},{36,28},{40,32... | collective-permute-start | bytes 4718600 | tf_op jit(solution)/shard_map/ppermute | solution.py:16
  860.7 80.8 %collective-permute-start.11 = (f32[12,512]{1,0:T(8,128)S(1)}, f32[12,512]{1,0:T(8,128)S(1)}, u32[]{:S(2)}, u32[]{:S(2)}) collective-permute-start(f32[12,512]{1,0:T(8,128)S(1)} %get-tuple-element.735), channel_id=1, source_target_pairs={{8,0},{12,4},{16,8},{20,12},{24,16},{28,20},{32,24},{36,28},{40,32... | collective-permute-start | bytes 73736 | tf_op jit(solution)/shard_map/ppermute | solution.py:16
  863.1 78.5 %collective-permute-start.9 = (f32[12,512]{1,0:T(8,128)S(1)}, f32[12,512]{1,0:T(8,128)S(1)}, u32[]{:S(2)}, u32[]{:S(2)}) collective-permute-start(f32[12,512]{1,0:T(8,128)S(1)} %get-tuple-element.734), channel_id=1, source_target_pairs={{8,0},{12,4},{16,8},{20,12},{24,16},{28,20},{32,24},{36,28},{40,32... | collective-permute-start | bytes 73736 | tf_op jit(solution)/shard_map/ppermute | solution.py:16
  1031.1 24.9 %all-to-all-start.2 = ((bf16[4,128,1536]{2,1,0:T(8,128)(2,1)}), bf16[4,128,1536]{2,1,0:T(8,128)(2,1)}, u32[]{:S(2)}, u32[]{:S(2)}) async-start(bf16[4,128,1536]{2,1,0:T(8,128)(2,1)} %bitcast.74), calls=%async_computation.2 | async-start | bytes 3145728 | tf_op jit(solution)/shard_map/all_to_all | solution.py:201
  1056.0 22.9 %all-to-all-start.1 = ((bf16[4,128,1536]{2,1,0:T(8,128)(2,1)}), bf16[4,128,1536]{2,1,0:T(8,128)(2,1)S(1)}, u32[]{:S(2)}, u32[]{:S(2)}) async-start(bf16[4,128,1536]{2,1,0:T(8,128)(2,1)} %bitcast.75), calls=%async_computation.1 | async-start | bytes 3145728 | tf_op jit(solution)/shard_map/all_to_all | solution.py:200
  (4 other events, 79.2 us)
Sparse Core Ops, SparseCore 0:
  90.5 69.9 all-gather.10
  163.3 62.3 all-gather.8
  238.6 62.3 all-gather.10
  303.7 62.3 all-gather.8
  379.0 62.3 all-gather.10
  444.1 62.3 all-gather.8
  519.3 62.3 all-gather.10
  584.6 62.3 all-gather.8
Sparse Core Ops, SparseCore 1:
  861.4 130.8 all-reduce.2
